TPU v7x, 32 devices: a whole 2x2x4 slice. The times are simulated.
32 devices in a mesh: groups: 2 (over y), ctx: 4 (over z), tp: 2 (over x), sub: 2 (over core).
Axes of the slice: x: 2, y: 2, z: 4, core: 2. Of those that a mesh axis runs over, the one named last changes fastest.
Arguments:
- queries: bfloat16 [3072, 8192], P(('groups', 'ctx'), ('tp', 'sub')), parts along dimension 0, may hold values from -200 to 200
- keys: bfloat16 [3072, 1024], P(('groups', 'ctx'), ('tp', 'sub')), parts along dimension 0, may hold values from -6 to 6
- values: bfloat16 [3072, 1024], P(('groups', 'ctx'), ('tp', 'sub')), parts along dimension 0, may hold values from -6 to 6
- segment_ids: int32 [3072], P(('groups', 'ctx')), parts along dimension 0, may hold values from 0 to 8, as said below
Outputs:
- attended: bfloat16 [3072, 8192], P(('groups', 'ctx'), ('tp', 'sub')), parts along dimension 0
There are 2 independent parts, one for each index of `groups`. A program takes and returns all parts, laid end to end along the dimension named above; each array names one. Nothing has to cross between parts.
Inputs may be any that keep to these rules, and one draw needn't show every extreme that they name: segment_ids is 0 on the first 384 tokens; after them exactly 8 chains 1, 2, ..., 8 follow in order and fill the row, each a run of 96 to 192 tokens, one of them exactly 192.
All inputs are finite; a program needn't handle non-finite values.
Results may differ from a plain program's by a relative error of at most 0.0041.
Values may be sent and summed in bfloat16 or wider, within the bound.
No kernel may reach another device: no remote copies, remote signals or barrier semaphores. Data moves between devices by JAX's collectives and lax.ppermute only.
A program may use at most 64 MiB of HBM per device.

v0:
```python
import jax
import jax.numpy as jnp
from jax import lax
from jax.sharding import PartitionSpec as P

HEAD_DIM = 128
GROUP = 8


def attend_block(
    running,
    key_block,
    value_block,
    segment_block,
    first_row,
    query_heads,
    query_places,
    query_segment,
):
    number = key_block.shape[0]
    heads_here = key_block.shape[1] // HEAD_DIM
    key_places = first_row + jnp.arange(number, dtype=jnp.int32)
    same = (segment_block[None, :] == query_segment[:, None]) | (segment_block[None, :] == 0)
    visible = (key_places[None, :] <= query_places[:, None]) & same
    key_heads = key_block.reshape(number, heads_here, HEAD_DIM)
    value_heads = value_block.reshape(number, heads_here, HEAD_DIM)

    def compute(state):
        row_peak, row_total, weighted = state
        scores = jnp.einsum(
            "qhgd,khd->hgqk", query_heads, key_heads, preferred_element_type=jnp.float32
        ) * HEAD_DIM ** (-0.5)
        scores = jnp.where(visible[None, None], scores, -1e30)
        new_peak = jnp.maximum(row_peak, jnp.max(scores, axis=-1))
        factor = jnp.exp(row_peak - new_peak)
        weights = jnp.where(visible[None, None], jnp.exp(scores - new_peak[..., None]), 0.0)
        new_total = row_total * factor + jnp.sum(weights, axis=-1)
        added = jnp.einsum(
            "hgqk,khd->hgqd",
            weights.astype(jnp.bfloat16),
            value_heads,
            preferred_element_type=jnp.float32,
        )
        return (new_peak, new_total, weighted * factor[..., None] + added)

    return lax.cond(jnp.any(visible), compute, lambda state: state, running)


def per_device(queries, keys, values, segment_ids):
    row_count = queries.shape[0]
    heads_here = keys.shape[1] // HEAD_DIM
    my_index = lax.axis_index("ctx")
    query_places = my_index * row_count + jnp.arange(row_count, dtype=jnp.int32)
    query_heads = queries.reshape(row_count, heads_here, GROUP, HEAD_DIM)
    initial = (
        jnp.full((heads_here, GROUP, row_count), -1e30, jnp.float32),
        jnp.zeros((heads_here, GROUP, row_count), jnp.float32),
        jnp.zeros((heads_here, GROUP, row_count, HEAD_DIM), jnp.float32),
    )
    key_all = lax.all_gather(keys, "ctx", axis=0, tiled=True)
    value_all = lax.all_gather(values, "ctx", axis=0, tiled=True)
    segment_all = lax.all_gather(segment_ids, "ctx", axis=0, tiled=True)
    blocks = max(1, key_all.shape[0] // row_count)
    width_rows = key_all.shape[0] // blocks

    def turn(number, state):
        offset = number * width_rows
        key_part = lax.dynamic_slice_in_dim(key_all, offset, width_rows, 0)
        value_part = lax.dynamic_slice_in_dim(value_all, offset, width_rows, 0)
        segment_part = lax.dynamic_slice_in_dim(segment_all, offset, width_rows, 0)
        return attend_block(
            state,
            key_part,
            value_part,
            segment_part,
            offset,
            query_heads,
            query_places,
            segment_ids,
        )

    final = lax.fori_loop(0, blocks, turn, initial)
    row_peak, row_total, weighted = final
    mixed = weighted / row_total[..., None]
    mixed = jnp.transpose(mixed, (2, 0, 1, 3)).reshape(row_count, heads_here * GROUP * HEAD_DIM)
    return mixed.astype(jnp.bfloat16)


def solution(mesh):
    placed = (
        P(("groups", "ctx"), ("tp", "sub")),
        P(("groups", "ctx"), ("tp", "sub")),
        P(("groups", "ctx"), ("tp", "sub")),
        P(("groups", "ctx")),
    )
    return jax.shard_map(
        per_device,
        mesh=mesh,
        in_specs=placed,
        out_specs=P(("groups", "ctx"), ("tp", "sub")),
        check_vma=False,
    )
```

profile of v0, /device:TPU:22, one launch (start us, length us, event | category | flops | bytes accessed | tf_op | source)
XLA Modules:
  0.0 98.1 jit_solution(1589817121826386383)
XLA Ops:
  0.0 0.7 reshape.39
  0.7 10.3 %all-gather = s32[4,1,384]{2,1,0:T(1,128)S(1)} all-gather(s32[1,1,384]{2,1,0:T(1,128)S(1)} %reshape.39), channel_id=1, replica_groups=mesh['groups'=2,'ctx'=4,'tp'=2,'sub'=2] {'ctx'}, dimensions={0}, use_global_device_ids=true | all-gather | bytes 7680 | tf_op jit(solution)/shard_map/all_gather | solution.py:62
  11.0 1.1 %copy.18 = bf16[384,256]{0,1:T(8,128)(2,1)S(1)} copy(bf16[384,256]{1,0:T(8,128)(2,1)} %param.9) | data formatting | bytes 393216 | tf_op args[1]
  12.1 1.1 %copy.20 = bf16[384,256]{0,1:T(8,128)(2,1)S(1)} copy(bf16[384,256]{1,0:T(8,128)(2,1)} %param.10) | data formatting | bytes 393216 | tf_op args[2]
  13.2 18.8 %all_gather.11 = bf16[1536,256]{0,1:T(8,128)(2,1)} all-gather(bf16[384,256]{0,1:T(8,128)(2,1)S(1)} %copy.20), channel_id=1, replica_groups=mesh['groups'=2,'ctx'=4,'tp'=2,'sub'=2] {'ctx'}, dimensions={0}, use_global_device_ids=true | all-gather | bytes 983040 | tf_op jit(solution)/shard_map/all_gather | solution.py:61
  32.0 17.9 %all_gather.10 = bf16[1536,256]{0,1:T(8,128)(2,1)} all-gather(bf16[384,256]{0,1:T(8,128)(2,1)S(1)} %copy.18), channel_id=1, replica_groups=mesh['groups'=2,'ctx'=4,'tp'=2,'sub'=2] {'ctx'}, dimensions={0}, use_global_device_ids=true | all-gather | bytes 983040 | tf_op jit(solution)/shard_map/all_gather | solution.py:60
  49.9 0.0 copy-start.2
  49.9 1.9 %copy.19 = bf16[384,2048]{0,1:T(8,128)(2,1)S(1)} copy(bf16[384,2048]{1,0:T(8,128)(2,1)} %param.8) | data formatting | bytes 3145728 | tf_op args[0]
  51.8 1.0 copy.21
  52.8 2.0 %broadcast_in_dim.53 = f32[2,8,384,128]{3,2,1,0:T(8,128)} broadcast(f32[]{:T(128)} %constant.68.clone.1), dimensions={} | broadcast | bytes 3145732 | tf_op jit(solution)/shard_map/broadcast_in_dim | solution.py:58
  54.8 0.0 copy-done.2
  54.8 38.4 %while.18 = (s32[]{:T(128)}, f32[2,8,384]{2,1,0:T(8,128)S(1)}, f32[2,8,384]{2,1,0:T(8,128)S(1)}, f32[2,8,384,128]{3,2,1,0:T(8,128)}, s32[1536]{0:T(1024)S(1)}, /...) while((s32[]{:T(128)}, f32[2,8,384]{2,1,0:T(8,128)S(1)}, ...), condition=%wide.region_6.7_spmd.clone, body=%wide.region_0.6_spmd.clone.sunk | while | flops 1240953984 | bytes 63517816 | solution.py:82
  54.8 0.1 broadcast_compare_fusion.2
  54.9 0.9 fusion.19
  56.4 10.6 %conditional.3 = ((f32[2,8,384]{2,1,0:T(8,128)S(1)}, f32[2,8,384]{2,1,0:T(8,128)S(1)}, f32[2,8,384,128]{3,2,1,0:T(8,128)})) conditional(s32[]{:T(128)} %convert_element_type.33, (f32[2,8,384]{2,1,0:T(8,128)S(1)}, f32[2,8,384]{2,1,0:T(8,128)S(1)}, f32[2,8,384,128]{3,2,1,0:T(8,128)}) %tuple.60, (pred[384,384]{0,1:T(8,128)(4,1)S(1)}, ...), branch_computations={%region_2.0_spmd, %region_3.5_spmd} | conditional | flops 1240215552 | bytes 63357020 | solution.py:46
  56.4 1.1 %constant_dynamic-slice_fusion = (bf16[384,256]{0,1:T(8,128)(2,1)S(1)}, bf16[384,256]{0,1:T(8,128)(2,1)S(1)}) fusion(bf16[1536,256]{0,1:T(8,128)(2,1)} %get-tuple-element.240, s32[]{:T(128)} %get-tuple-element.236, bf16[1536,256]{0,1:T(8,128)(2,1)} %get-tuple-element.235), kind=kLoop, calls=%fused_computation.11 | loop fusion | bytes 786436 | tf_op jit(solution)/shard_map/while/body/eval_jaxpr/dynamic_slice | solution.py:69
  57.5 1.7 %fusion.2 = (f32[2,8,384]{2,1,0:T(8,128)S(1)}, f32[2,384,384,8]{2,1,3,0:T(8,128)S(1)}) fusion(pred[384,384]{0,1:T(8,128)(4,1)S(1)} %get-tuple-element.234, bf16[384,2,128,1]{0,2,3,1:T(8,128)(2,1)S(1)} %bitcast.34, bf16[384,2,8,128]{3,0,2,1:T(8,128)(2,1)S(1)} %get-tuple-element.237), kind=kOutput, calls=%fused_computation.3 | convolution fusion | flops 611051520 | bytes 11378688 | tf_op jit(solution)/shard_map/while/body/eval_jaxpr/cond/branch_1_fun/qhgd,khd->hgqk/dot_general | solution.py:30
  59.2 0.0 copy-start
  59.2 2.3 %fusion.4 = f32[2,8,384]{2,1,0:T(8,128)S(1)} fusion(f32[2,384,384,8]{2,1,3,0:T(8,128)S(1)} %get-tuple-element.332, f32[2,8,384]{2,1,0:T(8,128)S(1)} %max.4, pred[384,384]{0,1:T(8,128)(4,1)S(1)} %get-tuple-element.234), kind=kLoop, calls=%fused_computation.5 | loop fusion | flops 11790336 | bytes 9633792 | tf_op jit(solution)/shard_map/while/body/eval_jaxpr/cond/branch_1_fun/reduce_sum | solution.py:37
  61.5 0.0 copy-done
  61.5 3.8 %multiply_add_fusion = f32[2,8,384,128]{3,2,1,0:T(8,128)S(1)} fusion(f32[2,8,384,128]{3,2,1,0:T(8,128)S(1)} %copy-done, bf16[384,2,128,1]{0,2,3,1:T(8,128)(2,1)S(1)} %bitcast.37, f32[2,384,384,8]{2,1,3,0:T(8,128)S(1)} %get-tuple-element.332, f32[2,8,384]{2,1,0:T(8,128)S(1)} %max.4, pred[384,384]{0,1:T(8,128)(4,1)S(1)} %get-tuple-element.234, ...), kind=kOutput, calls=%fused_computation.8 | convolution fusion | flops 617349120 | bytes 16121856 | tf_op jit(solution)/shard_map/while/body/eval_jaxpr/cond/branch_1_fun/hgqk,khd->hgqd/dot_general | solution.py:38
  65.4 0.0 copy-start.1
  65.4 1.6 %copy-done.1 = f32[2,8,384,128]{3,2,1,0:T(8,128)} copy-done((f32[2,8,384,128]{3,2,1,0:T(8,128)}, f32[2,8,384,128]{3,2,1,0:T(8,128)S(1)}, u32[]{:S(2)}) %copy-start.1) | copy-done | bytes 3145752 | tf_op jit(solution)/shard_map/while/body/eval_jaxpr/cond
  67.0 0.1 broadcast_compare_fusion.2
  67.1 0.9 fusion.19
  68.6 10.6 %conditional.3 = ((f32[2,8,384]{2,1,0:T(8,128)S(1)}, f32[2,8,384]{2,1,0:T(8,128)S(1)}, f32[2,8,384,128]{3,2,1,0:T(8,128)})) conditional(s32[]{:T(128)} %convert_element_type.33, (f32[2,8,384]{2,1,0:T(8,128)S(1)}, f32[2,8,384]{2,1,0:T(8,128)S(1)}, f32[2,8,384,128]{3,2,1,0:T(8,128)}) %tuple.60, (pred[384,384]{0,1:T(8,128)(4,1)S(1)}, ...), branch_computations={%region_2.0_spmd, %region_3.5_spmd} | conditional | flops 1240215552 | bytes 63357020 | solution.py:46
  68.6 1.1 %constant_dynamic-slice_fusion = (bf16[384,256]{0,1:T(8,128)(2,1)S(1)}, bf16[384,256]{0,1:T(8,128)(2,1)S(1)}) fusion(bf16[1536,256]{0,1:T(8,128)(2,1)} %get-tuple-element.240, s32[]{:T(128)} %get-tuple-element.236, bf16[1536,256]{0,1:T(8,128)(2,1)} %get-tuple-element.235), kind=kLoop, calls=%fused_computation.11 | loop fusion | bytes 786436 | tf_op jit(solution)/shard_map/while/body/eval_jaxpr/dynamic_slice | solution.py:69
  69.7 1.7 %fusion.2 = (f32[2,8,384]{2,1,0:T(8,128)S(1)}, f32[2,384,384,8]{2,1,3,0:T(8,128)S(1)}) fusion(pred[384,384]{0,1:T(8,128)(4,1)S(1)} %get-tuple-element.234, bf16[384,2,128,1]{0,2,3,1:T(8,128)(2,1)S(1)} %bitcast.34, bf16[384,2,8,128]{3,0,2,1:T(8,128)(2,1)S(1)} %get-tuple-element.237), kind=kOutput, calls=%fused_computation.3 | convolution fusion | flops 611051520 | bytes 11378688 | tf_op jit(solution)/shard_map/while/body/eval_jaxpr/cond/branch_1_fun/qhgd,khd->hgqk/dot_general | solution.py:30
  71.4 0.0 copy-start
  71.5 2.3 %fusion.4 = f32[2,8,384]{2,1,0:T(8,128)S(1)} fusion(f32[2,384,384,8]{2,1,3,0:T(8,128)S(1)} %get-tuple-element.332, f32[2,8,384]{2,1,0:T(8,128)S(1)} %max.4, pred[384,384]{0,1:T(8,128)(4,1)S(1)} %get-tuple-element.234), kind=kLoop, calls=%fused_computation.5 | loop fusion | flops 11790336 | bytes 9633792 | tf_op jit(solution)/shard_map/while/body/eval_jaxpr/cond/branch_1_fun/reduce_sum | solution.py:37
  73.8 0.0 copy-done
  73.8 3.8 %multiply_add_fusion = f32[2,8,384,128]{3,2,1,0:T(8,128)S(1)} fusion(f32[2,8,384,128]{3,2,1,0:T(8,128)S(1)} %copy-done, bf16[384,2,128,1]{0,2,3,1:T(8,128)(2,1)S(1)} %bitcast.37, f32[2,384,384,8]{2,1,3,0:T(8,128)S(1)} %get-tuple-element.332, f32[2,8,384]{2,1,0:T(8,128)S(1)} %max.4, pred[384,384]{0,1:T(8,128)(4,1)S(1)} %get-tuple-element.234, ...), kind=kOutput, calls=%fused_computation.8 | convolution fusion | flops 617349120 | bytes 16121856 | tf_op jit(solution)/shard_map/while/body/eval_jaxpr/cond/branch_1_fun/hgqk,khd->hgqd/dot_general | solution.py:38
  77.6 0.0 copy-start.1
  77.6 1.6 %copy-done.1 = f32[2,8,384,128]{3,2,1,0:T(8,128)} copy-done((f32[2,8,384,128]{3,2,1,0:T(8,128)}, f32[2,8,384,128]{3,2,1,0:T(8,128)S(1)}, u32[]{:S(2)}) %copy-start.1) | copy-done | bytes 3145752 | tf_op jit(solution)/shard_map/while/body/eval_jaxpr/cond
  79.3 0.1 broadcast_compare_fusion.2
  79.4 0.9 fusion.19
  80.9 10.6 %conditional.3 = ((f32[2,8,384]{2,1,0:T(8,128)S(1)}, f32[2,8,384]{2,1,0:T(8,128)S(1)}, f32[2,8,384,128]{3,2,1,0:T(8,128)})) conditional(s32[]{:T(128)} %convert_element_type.33, (f32[2,8,384]{2,1,0:T(8,128)S(1)}, f32[2,8,384]{2,1,0:T(8,128)S(1)}, f32[2,8,384,128]{3,2,1,0:T(8,128)}) %tuple.60, (pred[384,384]{0,1:T(8,128)(4,1)S(1)}, ...), branch_computations={%region_2.0_spmd, %region_3.5_spmd} | conditional | flops 1240215552 | bytes 63357020 | solution.py:46
  80.9 1.1 %constant_dynamic-slice_fusion = (bf16[384,256]{0,1:T(8,128)(2,1)S(1)}, bf16[384,256]{0,1:T(8,128)(2,1)S(1)}) fusion(bf16[1536,256]{0,1:T(8,128)(2,1)} %get-tuple-element.240, s32[]{:T(128)} %get-tuple-element.236, bf16[1536,256]{0,1:T(8,128)(2,1)} %get-tuple-element.235), kind=kLoop, calls=%fused_computation.11 | loop fusion | bytes 786436 | tf_op jit(solution)/shard_map/while/body/eval_jaxpr/dynamic_slice | solution.py:69
  82.0 1.7 %fusion.2 = (f32[2,8,384]{2,1,0:T(8,128)S(1)}, f32[2,384,384,8]{2,1,3,0:T(8,128)S(1)}) fusion(pred[384,384]{0,1:T(8,128)(4,1)S(1)} %get-tuple-element.234, bf16[384,2,128,1]{0,2,3,1:T(8,128)(2,1)S(1)} %bitcast.34, bf16[384,2,8,128]{3,0,2,1:T(8,128)(2,1)S(1)} %get-tuple-element.237), kind=kOutput, calls=%fused_computation.3 | convolution fusion | flops 611051520 | bytes 11378688 | tf_op jit(solution)/shard_map/while/body/eval_jaxpr/cond/branch_1_fun/qhgd,khd->hgqk/dot_general | solution.py:30
  83.7 0.0 copy-start
  83.7 2.3 %fusion.4 = f32[2,8,384]{2,1,0:T(8,128)S(1)} fusion(f32[2,384,384,8]{2,1,3,0:T(8,128)S(1)} %get-tuple-element.332, f32[2,8,384]{2,1,0:T(8,128)S(1)} %max.4, pred[384,384]{0,1:T(8,128)(4,1)S(1)} %get-tuple-element.234), kind=kLoop, calls=%fused_computation.5 | loop fusion | flops 11790336 | bytes 9633792 | tf_op jit(solution)/shard_map/while/body/eval_jaxpr/cond/branch_1_fun/reduce_sum | solution.py:37
  86.0 0.0 copy-done
  86.0 3.8 %multiply_add_fusion = f32[2,8,384,128]{3,2,1,0:T(8,128)S(1)} fusion(f32[2,8,384,128]{3,2,1,0:T(8,128)S(1)} %copy-done, bf16[384,2,128,1]{0,2,3,1:T(8,128)(2,1)S(1)} %bitcast.37, f32[2,384,384,8]{2,1,3,0:T(8,128)S(1)} %get-tuple-element.332, f32[2,8,384]{2,1,0:T(8,128)S(1)} %max.4, pred[384,384]{0,1:T(8,128)(4,1)S(1)} %get-tuple-element.234, ...), kind=kOutput, calls=%fused_computation.8 | convolution fusion | flops 617349120 | bytes 16121856 | tf_op jit(solution)/shard_map/while/body/eval_jaxpr/cond/branch_1_fun/hgqk,khd->hgqd/dot_general | solution.py:38
  89.9 0.0 copy-start.1
  89.9 1.6 %copy-done.1 = f32[2,8,384,128]{3,2,1,0:T(8,128)} copy-done((f32[2,8,384,128]{3,2,1,0:T(8,128)}, f32[2,8,384,128]{3,2,1,0:T(8,128)S(1)}, u32[]{:S(2)}) %copy-start.1) | copy-done | bytes 3145752 | tf_op jit(solution)/shard_map/while/body/eval_jaxpr/cond
  91.5 0.1 broadcast_compare_fusion.2
  91.6 0.9 fusion.19
  93.2 2.4 %fusion.13 = bf16[384,2,8,128]{3,0,2,1:T(8,128)(2,1)S(1)} fusion(f32[2,8,384,128]{3,2,1,0:T(8,128)} %get-tuple-element.257, f32[2,8,384]{2,1,0:T(8,128)S(1)} %get-tuple-element.258), kind=kLoop, calls=%fused_computation.22 | loop fusion | flops 1572864 | bytes 4743168 | tf_op jit(solution)/shard_map/convert_element_type | solution.py:86
  95.6 1.0 %copy.22 = bf16[384,2,8,128]{3,2,1,0:T(8,128)(2,1)S(1)} copy(bf16[384,2,8,128]{3,0,2,1:T(8,128)(2,1)S(1)} %fusion.13) | data formatting | bytes 3145728 | tf_op jit(solution)/shard_map/convert_element_type | solution.py:86
  96.6 1.6 %copy.32 = bf16[48,8,16,128]{3,1,2,0:T(8,128)(2,1)} copy(bf16[48,8,16,128]{3,2,1,0:T(8,128)(2,1)S(1)} %bitcast.35) | data formatting | bytes 3145728
  (18 shorter events, 0.1 us)
Async XLA Ops:
  49.9 4.9 %copy-start.2 = (s32[384]{0:T(512)S(1)}, s32[384]{0:T(512)}, u32[]{:S(2)}) copy-start(s32[384]{0:T(512)} %param.11) | copy-start | bytes 4612
  59.2 2.3 %copy-start = (f32[2,8,384,128]{3,2,1,0:T(8,128)S(1)}, f32[2,8,384,128]{3,2,1,0:T(8,128)}, u32[]{:S(2)}) copy-start(f32[2,8,384,128]{3,2,1,0:T(8,128)} %get-tuple-element.239) | copy-start | bytes 9437188 | tf_op jit(solution)/shard_map/while/body/eval_jaxpr/cond
  65.4 1.7 %copy-start.1 = (f32[2,8,384,128]{3,2,1,0:T(8,128)}, f32[2,8,384,128]{3,2,1,0:T(8,128)S(1)}, u32[]{:S(2)}) copy-start(f32[2,8,384,128]{3,2,1,0:T(8,128)S(1)} %multiply_add_fusion) | copy-start | bytes 9437188 | tf_op jit(solution)/shard_map/while/body/eval_jaxpr/cond
  71.4 2.3 %copy-start = (f32[2,8,384,128]{3,2,1,0:T(8,128)S(1)}, f32[2,8,384,128]{3,2,1,0:T(8,128)}, u32[]{:S(2)}) copy-start(f32[2,8,384,128]{3,2,1,0:T(8,128)} %get-tuple-element.239) | copy-start | bytes 9437188 | tf_op jit(solution)/shard_map/while/body/eval_jaxpr/cond
  77.6 1.7 %copy-start.1 = (f32[2,8,384,128]{3,2,1,0:T(8,128)}, f32[2,8,384,128]{3,2,1,0:T(8,128)S(1)}, u32[]{:S(2)}) copy-start(f32[2,8,384,128]{3,2,1,0:T(8,128)S(1)} %multiply_add_fusion) | copy-start | bytes 9437188 | tf_op jit(solution)/shard_map/while/body/eval_jaxpr/cond
  83.7 2.3 %copy-start = (f32[2,8,384,128]{3,2,1,0:T(8,128)S(1)}, f32[2,8,384,128]{3,2,1,0:T(8,128)}, u32[]{:S(2)}) copy-start(f32[2,8,384,128]{3,2,1,0:T(8,128)} %get-tuple-element.239) | copy-start | bytes 9437188 | tf_op jit(solution)/shard_map/while/body/eval_jaxpr/cond
  89.9 1.7 %copy-start.1 = (f32[2,8,384,128]{3,2,1,0:T(8,128)}, f32[2,8,384,128]{3,2,1,0:T(8,128)S(1)}, u32[]{:S(2)}) copy-start(f32[2,8,384,128]{3,2,1,0:T(8,128)S(1)} %multiply_add_fusion) | copy-start | bytes 9437188 | tf_op jit(solution)/shard_map/while/body/eval_jaxpr/cond
where the time goes:
time: 98.4 us; the launch traced here: 98.1 us
  blocking collectives  47 us (48%)
  local copies, waits for them, and re-layouts  18.5 us (19%)
  matrix products  16.6 us (17%)
  other arithmetic  13.2 us (13%)
  loops' own time  2.79 us (3%)
    all_gather x1, blocking collectives, per_device(): value_all = lax.all_gather(values, 'ctx', axis=0, tiled=True)  18.8 us
    all_gather x1, blocking collectives, per_device(): key_all = lax.all_gather(keys, 'ctx', axis=0, tiled=True)  17.9 us
    dot_general x3, matrix products, compute(): jnp.einsum('hgqk,khd->hgqd', weights.astype(jnp.bfloat16), value_heads, p...  11.5 us
    all_gather x1, blocking collectives, per_device(): segment_all = lax.all_gather(segment_ids, 'ctx', axis=0, tiled=True)  10.3 us
    unnamed x9, local copies, waits for them, and re-layouts  7.27 us
    reduce_sum x3, other arithmetic, compute(): new_total = row_total * factor + jnp.sum(weights, axis=-1)  6.83 us
    dot_general x3, matrix products, compute(): jnp.einsum('qhgd,khd->hgqk', query_heads, key_heads, preferred_element_ty...  5.11 us
    cond x15, local copies, waits for them, and re-layouts  4.98 us

commit v1 on v0

--- a/solution.py
+++ b/solution.py
@@ -57,7 +57,12 @@
         jnp.zeros((heads_here, GROUP, row_count), jnp.float32),
         jnp.zeros((heads_here, GROUP, row_count, HEAD_DIM), jnp.float32),
     )
-    key_all = lax.all_gather(keys, "ctx", axis=0, tiled=True)
+    ring = [keys]
+    for hop in range(3):
+        ring.append(lax.ppermute(ring[-1], "ctx", [(dev, (dev + 1) % 4) for dev in range(4)]))
+    key_all = jnp.roll(
+        jnp.concatenate(ring[::-1], axis=0), (lax.axis_index("ctx") + 1) * ring[0].shape[0], axis=0
+    )
     value_all = lax.all_gather(values, "ctx", axis=0, tiled=True)
     segment_all = lax.all_gather(segment_ids, "ctx", axis=0, tiled=True)
     blocks = max(1, key_all.shape[0] // row_count)

time: 98.4 us -> 91.4 us (0.929)
  blocking collectives: 47 us -> 30.4 us
  waiting for transfers between devices: 0 us -> 5.07 us
  starting transfers between devices: 0 us -> 4.46 us
    all_gather x1 -> x0, blocking collectives: 17.9 us -> none  [per_device(): key_all = lax.all_gather(keys, 'ctx', axis=0, tiled=True)]
    ppermute x0 -> x3, waiting for transfers between devices: none -> 5.07 us  [per_device(): lax.ppermute(ring[-1], 'ctx', [(dev, (dev + 1) % 4) for dev in range(4)])]
    ppermute x0 -> x3, starting transfers between devices: none -> 4.46 us  [per_device(): lax.ppermute(ring[-1], 'ctx', [(dev, (dev + 1) % 4) for dev in range(4)])]
    dynamic_slice x3, local copies, waits for them, and re-layouts: 3.21 us -> 0.15 us  [turn(): value_part = lax.dynamic_slice_in_dim(value_all, offset, width_rows, 0)]
    unnamed x9 -> x16, local copies, waits for them, and re-layouts: 7.27 us -> 10 us
    all_gather x1, blocking collectives: 10.3 us -> 11.5 us  [per_device(): segment_all = lax.all_gather(segment_ids, 'ctx', axis=0, tiled=True)]
  transfers between devices with their start and end apart: 0 -> 3, of which waited for: 0 -> 1; matrix products, arithmetic and copies ran while one was open for 0% -> 6% of each run, Pallas kernels for 0% -> 0%
where the time goes in v1:
time: 91.4 us; the launch traced here: 90.7 us
  blocking collectives  30.4 us (33%)
  local copies, waits for them, and re-layouts  18.5 us (20%)
  matrix products  16.4 us (18%)
  other arithmetic  13.2 us (14%)
  waiting for transfers between devices  5.07 us (6%)
  starting transfers between devices  4.46 us (5%)
  loops' own time  2.55 us (3%)
    all_gather x1, blocking collectives, per_device(): value_all = lax.all_gather(values, 'ctx', axis=0, tiled=True)  18.9 us
    all_gather x1, blocking collectives, per_device(): segment_all = lax.all_gather(segment_ids, 'ctx', axis=0, tiled=True)  11.5 us
    dot_general x3, matrix products, compute(): jnp.einsum('hgqk,khd->hgqd', weights.astype(jnp.bfloat16), value_heads, p...  11.3 us
    unnamed x16, local copies, waits for them, and re-layouts  10 us
    reduce_sum x3, other arithmetic, compute(): new_total = row_total * factor + jnp.sum(weights, axis=-1)  6.83 us
    dot_general x3, matrix products, compute(): jnp.einsum('qhgd,khd->hgqk', query_heads, key_heads, preferred_element_ty...  5.11 us
    ppermute x3, waiting for transfers between devices, per_device(): lax.ppermute(ring[-1], 'ctx', [(dev, (dev + 1) % 4) for dev in range(4)])  5.07 us
    cond x15, local copies, waits for them, and re-layouts  4.93 us
  transfers between devices with their start and end apart: 3, of which 1 were waited for; matrix products, arithmetic and copies ran while one was open for 6% of the time, Pallas kernels for 0%

profile of v1, /device:TPU:22, one launch (start us, length us, event | category | flops | bytes accessed | tf_op | source)
XLA Modules:
  0.0 90.7 jit_solution(17125387557320996801)
XLA Ops:
  0.0 1.1 %copy.20 = bf16[384,256]{0,1:T(8,128)(2,1)S(1)} copy(bf16[384,256]{1,0:T(8,128)(2,1)} %param.9) | data formatting | bytes 393216 | tf_op args[1]
  1.1 1.6 %collective-permute-start = (bf16[384,256]{0,1:T(8,128)(2,1)S(1)}, bf16[384,256]{0,1:T(8,128)(2,1)S(1)}, u32[]{:S(2)}, u32[]{:S(2)}) collective-permute-start(bf16[384,256]{0,1:T(8,128)(2,1)S(1)} %copy.20), channel_id=1, source_target_pairs={{0,4},{4,8},{8,12},{12,0},{1,5},{5,9},{9,13},{13,1},{2,6},{6,10},{... | collective-permute-start | bytes 589832 | tf_op jit(solution)/shard_map/ppermute | solution.py:62
  2.7 5.1 %collective-permute-done = bf16[384,256]{0,1:T(8,128)(2,1)S(1)} collective-permute-done((bf16[384,256]{0,1:T(8,128)(2,1)S(1)}, bf16[384,256]{0,1:T(8,128)(2,1)S(1)}, u32[]{:S(2)}, u32[]{:S(2)}) %collective-permute-start) | collective-permute-done | bytes 196640 | tf_op jit(solution)/shard_map/ppermute | solution.py:62
  7.8 1.6 %collective-permute-start.1 = (bf16[384,256]{0,1:T(8,128)(2,1)S(1)}, bf16[384,256]{0,1:T(8,128)(2,1)}, u32[]{:S(2)}, u32[]{:S(2)}) collective-permute-start(bf16[384,256]{0,1:T(8,128)(2,1)S(1)} %collective-permute-done), channel_id=1, source_target_pairs={{0,4},{4,8},{8,12},{12,0},{1,5},{5,9},{9,13},{13,1},{2,6},{6,10},{... | collective-permute-start | bytes 589832 | tf_op jit(solution)/shard_map/ppermute | solution.py:62
  9.4 0.7 reshape.39
  10.0 11.5 %all-gather = s32[4,1,384]{2,1,0:T(1,128)S(1)} all-gather(s32[1,1,384]{2,1,0:T(1,128)S(1)} %reshape.39), channel_id=1, replica_groups=mesh['groups'=2,'ctx'=4,'tp'=2,'sub'=2] {'ctx'}, dimensions={0}, use_global_device_ids=true | all-gather | bytes 7680 | tf_op jit(solution)/shard_map/all_gather | solution.py:67
  21.6 1.7 %copy.24 = bf16[384,256]{0,1:T(8,128)(2,1)} copy(bf16[384,256]{1,0:T(8,128)(2,1)} %param.10) | data formatting | bytes 393216 | tf_op args[2]
  23.3 1.9 %copy.23 = bf16[384,2048]{0,1:T(8,128)(2,1)S(1)} copy(bf16[384,2048]{1,0:T(8,128)(2,1)} %param.8) | data formatting | bytes 3145728 | tf_op args[0]
  25.2 1.0 %copy.25 = bf16[384,2,8,128]{3,0,2,1:T(8,128)(2,1)S(1)} copy(bf16[384,2,8,128]{0,3,2,1:T(8,128)(2,1)S(1)} %bitcast.36) | data formatting | bytes 3145728
  26.2 0.0 collective-permute-done.1
  26.2 1.3 %collective-permute-start.2 = (bf16[384,256]{0,1:T(8,128)(2,1)}, bf16[384,256]{0,1:T(8,128)(2,1)S(1)}, u32[]{:S(2)}, u32[]{:S(2)}) collective-permute-start(bf16[384,256]{0,1:T(8,128)(2,1)} %collective-permute-done.1), channel_id=1, source_target_pairs={{0,4},{4,8},{8,12},{12,0},{1,5},{5,9},{9,13},{13,1},{2,6},{6,10},{... | collective-permute-start | bytes 589832 | tf_op jit(solution)/shard_map/ppermute | solution.py:62
  27.4 18.9 %all_gather.7 = bf16[1536,256]{0,1:T(8,128)(2,1)S(1)} all-gather(bf16[384,256]{0,1:T(8,128)(2,1)} %copy.24), channel_id=1, replica_groups=mesh['groups'=2,'ctx'=4,'tp'=2,'sub'=2] {'ctx'}, dimensions={0}, use_global_device_ids=true | all-gather | bytes 983040 | tf_op jit(solution)/shard_map/all_gather | solution.py:66
  46.4 0.0 collective-permute-done.2
  46.4 1.0 %constant_dynamic-update-slice_fusion.6 = bf16[3072,256]{0,1:T(8,128)(2,1)S(1)} fusion(bf16[3072,256]{0,1:T(8,128)(2,1)S(1)} %constant_dynamic-update-slice_fusion.7, bf16[384,256]{0,1:T(8,128)(2,1)} %collective-permute-done.1), kind=kLoop, calls=%fused_computation.29 | loop fusion | bytes 393216
  47.5 0.0 copy-start.2
  47.5 1.0 %constant_dynamic-update-slice_fusion.2 = bf16[3072,256]{0,1:T(8,128)(2,1)S(1)} fusion(bf16[3072,256]{0,1:T(8,128)(2,1)S(1)} %constant_dynamic-update-slice_fusion.3, bf16[384,256]{0,1:T(8,128)(2,1)} %collective-permute-done.1), kind=kLoop, calls=%fused_computation.25 | loop fusion | bytes 393216
  48.6 0.3 constant_dynamic-slice_fusion.2
  49.0 2.0 %broadcast_in_dim.53 = f32[2,8,384,128]{3,2,1,0:T(8,128)} broadcast(f32[]{:T(128)} %constant.85.clone.1), dimensions={} | broadcast | bytes 3145732 | tf_op jit(solution)/shard_map/broadcast_in_dim | solution.py:58
  50.9 0.0 copy-done.2
  50.9 34.8 %while.18 = (s32[]{:T(128)}, f32[2,8,384]{2,1,0:T(8,128)S(1)}, f32[2,8,384]{2,1,0:T(8,128)S(1)}, f32[2,8,384,128]{3,2,1,0:T(8,128)}, s32[1536]{0:T(1024)S(1)}, /...) while((s32[]{:T(128)}, f32[2,8,384]{2,1,0:T(8,128)S(1)}, ...), condition=%wide.region_6.7_spmd.clone, body=%wide.region_0.6_spmd.clone.sunk | while | flops 1240953984 | bytes 63517816 | solution.py:87
  50.9 0.1 broadcast_compare_fusion.2
  51.0 0.9 fusion.19
  52.5 9.5 %conditional.3 = ((f32[2,8,384]{2,1,0:T(8,128)S(1)}, f32[2,8,384]{2,1,0:T(8,128)S(1)}, f32[2,8,384,128]{3,2,1,0:T(8,128)})) conditional(s32[]{:T(128)} %convert_element_type.33, (f32[2,8,384]{2,1,0:T(8,128)S(1)}, f32[2,8,384]{2,1,0:T(8,128)S(1)}, f32[2,8,384,128]{3,2,1,0:T(8,128)}) %tuple.60, (pred[384,384]{0,1:T(8,128)(4,1)S(1)}, ...), branch_computations={%region_2.2_spmd, %region_3.5_spmd} | conditional | flops 1240215552 | bytes 63357020 | solution.py:46
  52.5 0.1 constant_dynamic-slice_fusion
  52.5 1.7 %fusion.2 = (f32[2,8,384]{2,1,0:T(8,128)S(1)}, f32[2,384,384,8]{2,1,3,0:T(8,128)S(1)}) fusion(pred[384,384]{0,1:T(8,128)(4,1)S(1)} %get-tuple-element.234, bf16[384,2,128,1]{0,2,3,1:T(8,128)(2,1)S(1)} %bitcast.34, bf16[384,2,8,128]{3,0,2,1:T(8,128)(2,1)S(1)} %get-tuple-element.237), kind=kOutput, calls=%fused_computation.3 | convolution fusion | flops 611051520 | bytes 11378688 | tf_op jit(solution)/shard_map/while/body/eval_jaxpr/cond/branch_1_fun/qhgd,khd->hgqk/dot_general | solution.py:30
  54.3 0.0 copy-start
  54.3 2.3 %fusion.4 = f32[2,8,384]{2,1,0:T(8,128)S(1)} fusion(f32[2,384,384,8]{2,1,3,0:T(8,128)S(1)} %get-tuple-element.332, f32[2,8,384]{2,1,0:T(8,128)S(1)} %max.4, pred[384,384]{0,1:T(8,128)(4,1)S(1)} %get-tuple-element.234), kind=kLoop, calls=%fused_computation.5 | loop fusion | flops 11790336 | bytes 9633792 | tf_op jit(solution)/shard_map/while/body/eval_jaxpr/cond/branch_1_fun/reduce_sum | solution.py:37
  56.6 0.0 copy-done
  56.6 3.8 %multiply_add_fusion = f32[2,8,384,128]{3,2,1,0:T(8,128)S(1)} fusion(f32[2,8,384,128]{3,2,1,0:T(8,128)S(1)} %copy-done, bf16[384,2,128,1]{0,2,3,1:T(8,128)(2,1)S(1)} %bitcast.37, f32[2,384,384,8]{2,1,3,0:T(8,128)S(1)} %get-tuple-element.332, f32[2,8,384]{2,1,0:T(8,128)S(1)} %max.4, pred[384,384]{0,1:T(8,128)(4,1)S(1)} %get-tuple-element.234, ...), kind=kOutput, calls=%fused_computation.8 | convolution fusion | flops 617349120 | bytes 16121856 | tf_op jit(solution)/shard_map/while/body/eval_jaxpr/cond/branch_1_fun/hgqk,khd->hgqd/dot_general | solution.py:38
  60.4 0.0 copy-start.1
  60.4 1.6 %copy-done.1 = f32[2,8,384,128]{3,2,1,0:T(8,128)} copy-done((f32[2,8,384,128]{3,2,1,0:T(8,128)}, f32[2,8,384,128]{3,2,1,0:T(8,128)S(1)}, u32[]{:S(2)}) %copy-start.1) | copy-done | bytes 3145752 | tf_op jit(solution)/shard_map/while/body/eval_jaxpr/cond
  62.0 0.1 broadcast_compare_fusion.2
  62.1 0.9 fusion.19
  63.5 9.5 %conditional.3 = ((f32[2,8,384]{2,1,0:T(8,128)S(1)}, f32[2,8,384]{2,1,0:T(8,128)S(1)}, f32[2,8,384,128]{3,2,1,0:T(8,128)})) conditional(s32[]{:T(128)} %convert_element_type.33, (f32[2,8,384]{2,1,0:T(8,128)S(1)}, f32[2,8,384]{2,1,0:T(8,128)S(1)}, f32[2,8,384,128]{3,2,1,0:T(8,128)}) %tuple.60, (pred[384,384]{0,1:T(8,128)(4,1)S(1)}, ...), branch_computations={%region_2.2_spmd, %region_3.5_spmd} | conditional | flops 1240215552 | bytes 63357020 | solution.py:46
  63.6 0.1 constant_dynamic-slice_fusion
  63.6 1.7 %fusion.2 = (f32[2,8,384]{2,1,0:T(8,128)S(1)}, f32[2,384,384,8]{2,1,3,0:T(8,128)S(1)}) fusion(pred[384,384]{0,1:T(8,128)(4,1)S(1)} %get-tuple-element.234, bf16[384,2,128,1]{0,2,3,1:T(8,128)(2,1)S(1)} %bitcast.34, bf16[384,2,8,128]{3,0,2,1:T(8,128)(2,1)S(1)} %get-tuple-element.237), kind=kOutput, calls=%fused_computation.3 | convolution fusion | flops 611051520 | bytes 11378688 | tf_op jit(solution)/shard_map/while/body/eval_jaxpr/cond/branch_1_fun/qhgd,khd->hgqk/dot_general | solution.py:30
  65.3 0.0 copy-start
  65.3 2.3 %fusion.4 = f32[2,8,384]{2,1,0:T(8,128)S(1)} fusion(f32[2,384,384,8]{2,1,3,0:T(8,128)S(1)} %get-tuple-element.332, f32[2,8,384]{2,1,0:T(8,128)S(1)} %max.4, pred[384,384]{0,1:T(8,128)(4,1)S(1)} %get-tuple-element.234), kind=kLoop, calls=%fused_computation.5 | loop fusion | flops 11790336 | bytes 9633792 | tf_op jit(solution)/shard_map/while/body/eval_jaxpr/cond/branch_1_fun/reduce_sum | solution.py:37
  67.7 0.0 copy-done
  67.7 3.8 %multiply_add_fusion = f32[2,8,384,128]{3,2,1,0:T(8,128)S(1)} fusion(f32[2,8,384,128]{3,2,1,0:T(8,128)S(1)} %copy-done, bf16[384,2,128,1]{0,2,3,1:T(8,128)(2,1)S(1)} %bitcast.37, f32[2,384,384,8]{2,1,3,0:T(8,128)S(1)} %get-tuple-element.332, f32[2,8,384]{2,1,0:T(8,128)S(1)} %max.4, pred[384,384]{0,1:T(8,128)(4,1)S(1)} %get-tuple-element.234, ...), kind=kOutput, calls=%fused_computation.8 | convolution fusion | flops 617349120 | bytes 16121856 | tf_op jit(solution)/shard_map/while/body/eval_jaxpr/cond/branch_1_fun/hgqk,khd->hgqd/dot_general | solution.py:38
  71.4 0.0 copy-start.1
  71.4 1.6 %copy-done.1 = f32[2,8,384,128]{3,2,1,0:T(8,128)} copy-done((f32[2,8,384,128]{3,2,1,0:T(8,128)}, f32[2,8,384,128]{3,2,1,0:T(8,128)S(1)}, u32[]{:S(2)}) %copy-start.1) | copy-done | bytes 3145752 | tf_op jit(solution)/shard_map/while/body/eval_jaxpr/cond
  73.1 0.1 broadcast_compare_fusion.2
  73.2 0.9 fusion.19
  74.6 9.5 %conditional.3 = ((f32[2,8,384]{2,1,0:T(8,128)S(1)}, f32[2,8,384]{2,1,0:T(8,128)S(1)}, f32[2,8,384,128]{3,2,1,0:T(8,128)})) conditional(s32[]{:T(128)} %convert_element_type.33, (f32[2,8,384]{2,1,0:T(8,128)S(1)}, f32[2,8,384]{2,1,0:T(8,128)S(1)}, f32[2,8,384,128]{3,2,1,0:T(8,128)}) %tuple.60, (pred[384,384]{0,1:T(8,128)(4,1)S(1)}, ...), branch_computations={%region_2.2_spmd, %region_3.5_spmd} | conditional | flops 1240215552 | bytes 63357020 | solution.py:46
  74.6 0.1 constant_dynamic-slice_fusion
  74.7 1.7 %fusion.2 = (f32[2,8,384]{2,1,0:T(8,128)S(1)}, f32[2,384,384,8]{2,1,3,0:T(8,128)S(1)}) fusion(pred[384,384]{0,1:T(8,128)(4,1)S(1)} %get-tuple-element.234, bf16[384,2,128,1]{0,2,3,1:T(8,128)(2,1)S(1)} %bitcast.34, bf16[384,2,8,128]{3,0,2,1:T(8,128)(2,1)S(1)} %get-tuple-element.237), kind=kOutput, calls=%fused_computation.3 | convolution fusion | flops 611051520 | bytes 11378688 | tf_op jit(solution)/shard_map/while/body/eval_jaxpr/cond/branch_1_fun/qhgd,khd->hgqk/dot_general | solution.py:30
  76.4 0.0 copy-start
  76.4 2.3 %fusion.4 = f32[2,8,384]{2,1,0:T(8,128)S(1)} fusion(f32[2,384,384,8]{2,1,3,0:T(8,128)S(1)} %get-tuple-element.332, f32[2,8,384]{2,1,0:T(8,128)S(1)} %max.4, pred[384,384]{0,1:T(8,128)(4,1)S(1)} %get-tuple-element.234), kind=kLoop, calls=%fused_computation.5 | loop fusion | flops 11790336 | bytes 9633792 | tf_op jit(solution)/shard_map/while/body/eval_jaxpr/cond/branch_1_fun/reduce_sum | solution.py:37
  78.7 0.0 copy-done
  78.7 3.8 %multiply_add_fusion = f32[2,8,384,128]{3,2,1,0:T(8,128)S(1)} fusion(f32[2,8,384,128]{3,2,1,0:T(8,128)S(1)} %copy-done, bf16[384,2,128,1]{0,2,3,1:T(8,128)(2,1)S(1)} %bitcast.37, f32[2,384,384,8]{2,1,3,0:T(8,128)S(1)} %get-tuple-element.332, f32[2,8,384]{2,1,0:T(8,128)S(1)} %max.4, pred[384,384]{0,1:T(8,128)(4,1)S(1)} %get-tuple-element.234, ...), kind=kOutput, calls=%fused_computation.8 | convolution fusion | flops 617349120 | bytes 16121856 | tf_op jit(solution)/shard_map/while/body/eval_jaxpr/cond/branch_1_fun/hgqk,khd->hgqd/dot_general | solution.py:38
  82.5 0.0 copy-start.1
  82.5 1.6 %copy-done.1 = f32[2,8,384,128]{3,2,1,0:T(8,128)} copy-done((f32[2,8,384,128]{3,2,1,0:T(8,128)}, f32[2,8,384,128]{3,2,1,0:T(8,128)S(1)}, u32[]{:S(2)}) %copy-start.1) | copy-done | bytes 3145752 | tf_op jit(solution)/shard_map/while/body/eval_jaxpr/cond
  84.1 0.1 broadcast_compare_fusion.2
  84.2 0.9 fusion.19
  85.7 2.4 %fusion.13 = bf16[384,2,8,128]{3,0,2,1:T(8,128)(2,1)S(1)} fusion(f32[2,8,384,128]{3,2,1,0:T(8,128)} %get-tuple-element.257, f32[2,8,384]{2,1,0:T(8,128)S(1)} %get-tuple-element.258), kind=kLoop, calls=%fused_computation.22 | loop fusion | flops 1572864 | bytes 4743168 | tf_op jit(solution)/shard_map/convert_element_type | solution.py:91
  88.1 1.0 %copy.26 = bf16[384,2,8,128]{3,2,1,0:T(8,128)(2,1)S(1)} copy(bf16[384,2,8,128]{3,0,2,1:T(8,128)(2,1)S(1)} %fusion.13) | data formatting | bytes 3145728 | tf_op jit(solution)/shard_map/convert_element_type | solution.py:91
  89.1 1.6 %copy.36 = bf16[48,8,16,128]{3,1,2,0:T(8,128)(2,1)} copy(bf16[48,8,16,128]{3,2,1,0:T(8,128)(2,1)S(1)} %bitcast.35) | data formatting | bytes 3145728
  (24 shorter events, 0.4 us)
Async XLA Ops:
  1.1 6.7 %collective-permute-start = (bf16[384,256]{0,1:T(8,128)(2,1)S(1)}, bf16[384,256]{0,1:T(8,128)(2,1)S(1)}, u32[]{:S(2)}, u32[]{:S(2)}) collective-permute-start(bf16[384,256]{0,1:T(8,128)(2,1)S(1)} %copy.20), channel_id=1, source_target_pairs={{0,4},{4,8},{8,12},{12,0},{1,5},{5,9},{9,13},{13,1},{2,6},{6,10},{... | collective-permute-start | bytes 589832 | tf_op jit(solution)/shard_map/ppermute | solution.py:62
  7.8 18.4 %collective-permute-start.1 = (bf16[384,256]{0,1:T(8,128)(2,1)S(1)}, bf16[384,256]{0,1:T(8,128)(2,1)}, u32[]{:S(2)}, u32[]{:S(2)}) collective-permute-start(bf16[384,256]{0,1:T(8,128)(2,1)S(1)} %collective-permute-done), channel_id=1, source_target_pairs={{0,4},{4,8},{8,12},{12,0},{1,5},{5,9},{9,13},{13,1},{2,6},{6,10},{... | collective-permute-start | bytes 589832 | tf_op jit(solution)/shard_map/ppermute | solution.py:62
  26.2 20.2 %collective-permute-start.2 = (bf16[384,256]{0,1:T(8,128)(2,1)}, bf16[384,256]{0,1:T(8,128)(2,1)S(1)}, u32[]{:S(2)}, u32[]{:S(2)}) collective-permute-start(bf16[384,256]{0,1:T(8,128)(2,1)} %collective-permute-done.1), channel_id=1, source_target_pairs={{0,4},{4,8},{8,12},{12,0},{1,5},{5,9},{9,13},{13,1},{2,6},{6,10},{... | collective-permute-start | bytes 589832 | tf_op jit(solution)/shard_map/ppermute | solution.py:62
  47.5 3.5 %copy-start.2 = (s32[384]{0:T(512)S(1)}, s32[384]{0:T(512)}, u32[]{:S(2)}) copy-start(s32[384]{0:T(512)} %param.11) | copy-start | bytes 4612
  54.3 2.3 %copy-start = (f32[2,8,384,128]{3,2,1,0:T(8,128)S(1)}, f32[2,8,384,128]{3,2,1,0:T(8,128)}, u32[]{:S(2)}) copy-start(f32[2,8,384,128]{3,2,1,0:T(8,128)} %get-tuple-element.239) | copy-start | bytes 9437188 | tf_op jit(solution)/shard_map/while/body/eval_jaxpr/cond
  60.4 1.6 %copy-start.1 = (f32[2,8,384,128]{3,2,1,0:T(8,128)}, f32[2,8,384,128]{3,2,1,0:T(8,128)S(1)}, u32[]{:S(2)}) copy-start(f32[2,8,384,128]{3,2,1,0:T(8,128)S(1)} %multiply_add_fusion) | copy-start | bytes 9437188 | tf_op jit(solution)/shard_map/while/body/eval_jaxpr/cond
  65.3 2.3 %copy-start = (f32[2,8,384,128]{3,2,1,0:T(8,128)S(1)}, f32[2,8,384,128]{3,2,1,0:T(8,128)}, u32[]{:S(2)}) copy-start(f32[2,8,384,128]{3,2,1,0:T(8,128)} %get-tuple-element.239) | copy-start | bytes 9437188 | tf_op jit(solution)/shard_map/while/body/eval_jaxpr/cond
  71.4 1.6 %copy-start.1 = (f32[2,8,384,128]{3,2,1,0:T(8,128)}, f32[2,8,384,128]{3,2,1,0:T(8,128)S(1)}, u32[]{:S(2)}) copy-start(f32[2,8,384,128]{3,2,1,0:T(8,128)S(1)} %multiply_add_fusion) | copy-start | bytes 9437188 | tf_op jit(solution)/shard_map/while/body/eval_jaxpr/cond
  76.4 2.3 %copy-start = (f32[2,8,384,128]{3,2,1,0:T(8,128)S(1)}, f32[2,8,384,128]{3,2,1,0:T(8,128)}, u32[]{:S(2)}) copy-start(f32[2,8,384,128]{3,2,1,0:T(8,128)} %get-tuple-element.239) | copy-start | bytes 9437188 | tf_op jit(solution)/shard_map/while/body/eval_jaxpr/cond
  82.5 1.6 %copy-start.1 = (f32[2,8,384,128]{3,2,1,0:T(8,128)}, f32[2,8,384,128]{3,2,1,0:T(8,128)S(1)}, u32[]{:S(2)}) copy-start(f32[2,8,384,128]{3,2,1,0:T(8,128)S(1)} %multiply_add_fusion) | copy-start | bytes 9437188 | tf_op jit(solution)/shard_map/while/body/eval_jaxpr/cond
